TPU v7x, 32 devices: a whole 2x2x4 slice. The times are simulated.
32 devices in a mesh: lat: 8 (over y, x, core), lon: 4 (over z).
Axes of the slice: x: 2, y: 2, z: 4, core: 2. Of those that a mesh axis runs over, the one named last changes fastest.
Arguments:
- tracer: float32 [16, 64, 2880], P(None, 'lat', 'lon'), may hold values from -6 to 6
- zonal_courant: float32 [16, 64, 2880], P(None, 'lat', 'lon'), may hold values from -0.35 to 0.35
- north_courant: float32 [16, 64, 2880], P(None, 'lat', 'lon'), may hold values from -0.35 to 0.35
- cutoff: int32 [16], replicated, may hold values from 1 to 128
Outputs:
- advanced: float32 [16, 64, 2880], P(None, 'lat', 'lon')
All inputs are finite; a program needn't handle non-finite values.
Results may differ from a plain program's by a relative error of at most 0.0001.
Values sent between devices are 32-bit elements; how exact they have to be, the bound alone decides.
A program may use at most 64 MiB of HBM per device.

v0:
```python
import functools
import math

import jax
import jax.numpy as jnp
import numpy as np
from jax import lax
from jax.experimental import pallas as pl
from jax.experimental.pallas import tpu as pltpu
from jax.sharding import PartitionSpec as P

KMAX = 128
DIFFUSION = 0.2
LANES = 128
MESH = pl.DeviceIdType.MESH
F32 = jnp.float32
BF16 = jnp.bfloat16


def split_table(table):
    high = table.astype(np.float32).astype(BF16)
    low = (table - high.astype(np.float64)).astype(np.float32).astype(BF16)
    return np.stack([high, low])


def trig(columns, total):
    modes = np.arange(KMAX)
    angle = (columns[:, None] * modes[None, :] % total) * (2.0 * math.pi / total)
    return np.concatenate([np.cos(angle), np.sin(angle)], axis=1)


def window_basis(cols, total):
    bandwidth = (KMAX - 0.5) / total
    place = np.arange(cols)
    operator = np.diag(((cols - 1 - 2 * place) / 2.0) ** 2 * math.cos(2.0 * math.pi * bandwidth))
    beside = np.arange(1, cols) * (cols - np.arange(1, cols)) / 2.0
    operator = operator + np.diag(beside, 1) + np.diag(beside, -1)
    vectors = np.linalg.eigh(operator)[1][:, ::-1]
    half = vectors[:(cols + 1) // 2]
    peak = np.take_along_axis(half, np.abs(half).argmax(0)[None], 0)[0]
    return vectors * np.where(peak < 0, -1.0, 1.0)


def tables(cols, width, lon_count):
    total = cols * lon_count
    kept = min(LANES, cols)
    basis = np.zeros((width, LANES))
    basis[:cols, :kept] = window_basis(cols, total)[:, :kept]
    analysis = np.concatenate(list(split_table(basis)), axis=1)
    expand = np.zeros((lon_count, LANES, 2 * KMAX))
    for step in range(lon_count):
        expand[step] = basis[:cols].T @ trig(np.arange(cols) + step * cols, total)
    expand = split_table(expand.reshape(lon_count * LANES, 2 * KMAX))
    lane = np.arange(width)
    lane = np.where(lane == width - 1, -1, lane)
    synthesis = split_table(trig(lane, total).T.copy())
    ends = np.zeros((lon_count, 8, 2 * KMAX), np.float32)
    ends[:, 0] = trig(np.arange(lon_count) * cols, total)
    ends[:, 1] = trig(np.arange(lon_count) * cols + cols - 1, total)
    return analysis, expand, synthesis, ends


def split(value):
    high = value.astype(BF16)
    low = (value - high.astype(F32)).astype(BF16)
    return high, low


def dot3(value, table):
    high, low = split(value)
    t_high = table[0]
    t_low = table[1]
    dot = functools.partial(jnp.dot, preferred_element_type=F32)
    return dot(high, t_high) + (dot(low, t_high) + dot(high, t_low))


def dot_pair(value, table):
    size = value.shape[0]
    both = jnp.dot(jnp.concatenate(split(value), axis=0), table[...], preferred_element_type=F32)
    return both[:size, :LANES] + (both[:size, LANES:] + both[size:, :LANES])


def kernel(
    lat_count, lon_count, cap_blocks,
    cut_ref, tracer, zonal, north, ana_hbm, exp_hbm, syn_hbm, ends_hbm, out,
    q_in, zc, nc, ana, exp, syn, ends, q, tend,
    row_first, row_second, col_out, col_in, part, extra,
    load_sem, row_send, row_recv, col_send, col_recv, sum_send, sum_recv,
):
    rows, levels, cols = q_in.shape
    width = q.shape[2]
    total = cols * lon_count
    lat = lax.axis_index("lat")
    lon = lax.axis_index("lon")
    polar = jnp.logical_or(lat < cap_blocks, lat >= lat_count - cap_blocks)
    first = lat == 0
    last = lat == lat_count - 1
    east = lax.rem(lon + 1, lon_count)
    west = lax.rem(lon + lon_count - 1, lon_count)
    across = lax.rem(lon + lon_count // 2, lon_count)
    peers = [lax.rem(lon + step, lon_count) for step in range(lon_count)]
    steps = range(1, lon_count)
    order = [0, rows - 1, 1, rows - 2] + list(range(2, rows - 2))
    pieces = (((2, rows), (0, 2)), ((4, rows), (0, 4)))

    loads = []
    for index, (source, target) in enumerate(((tracer, q_in), (zonal, zc), (north, nc))):
        for row in range(rows):
            loads.append(pltpu.make_async_copy(
                source.at[:, row, :], target.at[row], load_sem.at[index * rows + row]))
    for load in loads[:rows]:
        load.start()

    barrier = pltpu.get_barrier_semaphore()

    def greet(there):
        pl.semaphore_signal(barrier, inc=1, device_id=there, device_id_type=MESH)

    @pl.when(jnp.logical_not(first))
    def _():
        greet({"lat": lat - 1, "lon": lon})

    @pl.when(jnp.logical_not(last))
    def _():
        greet({"lat": lat + 1, "lon": lon})

    @pl.when(polar)
    def _():
        for step in steps:
            greet({"lat": lat, "lon": peers[step]})

    @pl.when(jnp.logical_not(polar))
    def _():
        greet({"lat": lat, "lon": east})
        greet({"lat": lat, "lon": west})

    for load in loads[rows:]:
        load.start()
    tables_in = [
        pltpu.make_async_copy(ana_hbm, ana, load_sem.at[3 * rows]),
        pltpu.make_async_copy(exp_hbm, exp, load_sem.at[3 * rows + 1]),
        pltpu.make_async_copy(syn_hbm, syn, load_sem.at[3 * rows + 2]),
        pltpu.make_async_copy(ends_hbm, ends, load_sem.at[3 * rows + 3]),
    ]
    for load in tables_in:
        load.start()

    edge = first.astype(jnp.int32) + last.astype(jnp.int32)
    sides = jnp.where(polar, lon_count - 1, 2)
    pl.semaphore_wait(barrier, 2 - edge + sides)

    def row_copy(turn, slot, row, there):
        source = tracer.at[:, row, :] if turn == 0 else q.at[row]
        target = row_first if turn == 0 else row_second
        return pltpu.make_async_remote_copy(
            source, target.at[slot],
            row_send.at[turn, 0 if row else 1], row_recv.at[turn, slot],
            device_id=there, device_id_type=MESH)

    def to_north(turn):
        return row_copy(turn, 0, rows - 1, {"lat": lat + 1, "lon": lon})

    def to_south(turn):
        return row_copy(turn, 1, 0, {"lat": lat - 1, "lon": lon})

    def over_north():
        return row_copy(0, 1, rows - 1, {"lat": lat, "lon": across})

    def over_south():
        return row_copy(0, 0, 0, {"lat": lat, "lon": across})

    @pl.when(last)
    def _():
        over_north().start()

    @pl.when(first)
    def _():
        over_south().start()

    @pl.when(jnp.logical_not(last))
    def _():
        to_north(0).start()

    @pl.when(jnp.logical_not(first))
    def _():
        to_south(0).start()

    def rows_arrive(turn):
        @pl.when(jnp.logical_not(last))
        def _():
            to_south(turn).wait_recv()
            to_north(turn).wait_send()

        @pl.when(jnp.logical_not(first))
        def _():
            to_north(turn).wait_recv()
            to_south(turn).wait_send()

    def poles_arrive():
        @pl.when(last)
        def _():
            over_north().wait()

        @pl.when(first)
        def _():
            over_south().wait()

    lane = lax.broadcasted_iota(jnp.int32, (levels, LANES), 1)
    end_tile = (cols - 1) // LANES * LANES
    end_lane = (cols - 1) % LANES
    east_tile = cols // LANES * LANES
    west_tile = width - LANES

    def pack_cols(turn):
        packed = jnp.zeros((levels, LANES), F32)

        def put(packed, at, tile, came_from):
            return jnp.where(lane == at, pltpu.roll(tile, (at - came_from) % LANES, 1), packed)

        for row in range(rows):
            packed = put(packed, row, q[row, :, end_tile:end_tile + LANES], end_lane)
            packed = put(packed, rows + row, q[row, :, 0:LANES], 0)
        return packed

    def pack_factors(packed):
        for row in range(rows):
            tile = zc[row, :, end_tile:cols]
            if cols - end_tile < LANES:
                tile = jnp.concatenate(
                    [tile, jnp.zeros((levels, LANES - cols + end_tile), F32)], axis=1)
            factor = DIFFUSION - 0.5 * tile
            packed = jnp.where(
                lane == 2 * rows + row,
                pltpu.roll(factor, (2 * rows + row - end_lane) % LANES, 1), packed)
            factor = DIFFUSION + 0.5 * zc[row, :, 0:LANES]
            packed = jnp.where(
                lane == 3 * rows + row, pltpu.roll(factor, 3 * rows + row, 1), packed)
        return packed

    def place_cols(turn):
        from_west = col_in[turn, lon_count - 1]
        from_east = col_in[turn, 1]
        for row in range(rows):
            tile = q[row, :, east_tile:east_tile + LANES]
            moved = pltpu.roll(from_east, (cols % LANES - rows - row) % LANES, 1)
            q[row, :, east_tile:east_tile + LANES] = jnp.where(lane == cols % LANES, moved, tile)
            tile = q[row, :, west_tile:west_tile + LANES]
            moved = pltpu.roll(from_west, (LANES - 1 - row) % LANES, 1)
            q[row, :, west_tile:west_tile + LANES] = jnp.where(lane == LANES - 1, moved, tile)

    def col_copy(turn, step):
        return pltpu.make_async_remote_copy(
            col_out.at[turn], col_in.at[turn, lon_count - step],
            col_send.at[turn, step], col_recv.at[turn, lon_count - step],
            device_id={"lat": lat, "lon": peers[step]}, device_id_type=MESH)

    def col_arrival(turn, step):
        theirs = col_in.at[turn, step]
        return pltpu.make_async_remote_copy(
            theirs, theirs, col_send.at[turn, step], col_recv.at[turn, step],
            device_id={"lat": lat, "lon": peers[step]}, device_id_type=MESH)

    def sum_copy(turn, piece, step):
        low, high = pieces[turn][piece]
        return pltpu.make_async_remote_copy(
            part.at[turn, 0, low:high], part.at[turn, lon_count - step, low:high],
            sum_send.at[turn, piece, step], sum_recv.at[turn, piece, lon_count - step],
            device_id={"lat": lat, "lon": peers[step]}, device_id_type=MESH)

    def sum_arrival(turn, piece, step):
        low, high = pieces[turn][piece]
        theirs = part.at[turn, step, low:high]
        return pltpu.make_async_remote_copy(
            theirs, theirs, sum_send.at[turn, piece, step], sum_recv.at[turn, piece, step],
            device_id={"lat": lat, "lon": peers[step]}, device_id_type=MESH)

    def farthest_first(send):
        for distance in range(lon_count - 1, 0, -1):
            @pl.when(lon + distance < lon_count)
            def _():
                send(distance)

            @pl.when(lon - distance >= 0)
            def _():
                send(lon_count - distance)

    def stencil(turn, row):
        beyond = row_first if turn == 0 else row_second
        here = q[row]
        to_east = pltpu.roll(here, width - 1, 1)[:, :cols]
        to_west = pltpu.roll(here, 1, 1)[:, :cols]
        here = here[:, :cols]
        up = q[row + 1, :, :cols] if row < rows - 1 else beyond[1, :, :cols]
        down = q[row - 1, :, :cols] if row else beyond[0, :, :cols]
        return (-0.5 * zc[row] * (to_east - to_west)
                - 0.5 * nc[row] * (up - down)
                + DIFFUSION * (to_east + to_west + up + down - 4.0 * here))

    q[:, :, (width - LANES):] = jnp.zeros((rows, levels, LANES), F32)
    for load in loads[:rows]:
        load.wait()
    for row in range(rows):
        q[row, :, :cols] = q_in[row]

    @pl.when(jnp.logical_not(polar))
    def _():
        col_out[0] = pack_cols(0)
        for side in (1, lon_count - 1):
            col_copy(0, side).start()
        for load in loads[rows:] + tables_in:
            load.wait()
        for side in (1, lon_count - 1):
            col_arrival(0, side).wait_recv()
        place_cols(0)
        rows_arrive(0)
        for row in range(rows):
            tend[row, :, :cols] = stencil(0, row)
        for row in range(rows):
            q[row, :, :cols] = q[row, :, :cols] + tend[row, :, :cols]
        to_north(1).start()
        to_south(1).start()
        col_out[1] = pack_cols(1)
        for side in (1, lon_count - 1):
            col_copy(1, side).start()
        for side in (1, lon_count - 1):
            col_arrival(1, side).wait_recv()
        rows_arrive(1)
        place_cols(1)
        for row in range(rows):
            out[:, row, :] = q[row, :, :cols] + stencil(1, row)
        for turn in range(2):
            for side in (1, lon_count - 1):
                col_copy(turn, side).wait_send()

    @pl.when(polar)
    def _():
        tend[:, :, (width - LANES):] = jnp.zeros((rows, levels, LANES), F32)
        for load in loads[rows:2 * rows]:
            load.wait()
        col_out[0] = pack_factors(pack_cols(0))
        farthest_first(lambda step: col_copy(0, step).start())
        for load in loads[2 * rows:] + tables_in:
            load.wait()

        offset = jnp.where(
            lat < cap_blocks, lat * rows, (lat - lat_count + 2 * cap_blocks) * rows)
        mode = lax.broadcasted_iota(jnp.int32, (1, 2 * KMAX), 1) % KMAX
        weight = jnp.where(mode == 0, 1.0 / total, 2.0 / total).astype(F32)
        keep = [jnp.where(mode < cut_ref[offset + row], weight, 0.0) for row in range(rows)]
        parity = 1.0 - 2.0 * (lax.broadcasted_iota(jnp.int32, (1, 2 * KMAX), 1) % 2).astype(F32)

        def analyse(turn, piece):
            low, high = pieces[turn][piece]
            count = high - low
            for slot in range(low, high):
                tend[slot, :, :cols] = stencil(turn, order[slot])
            found = dot_pair(tend[low:high].reshape(count * levels, width), ana)
            part[turn, 0, low:high] = found.reshape(count, levels, LANES)
            farthest_first(lambda step: sum_copy(turn, piece, step).start())

        def collect(turn, piece):
            low, high = pieces[turn][piece]
            for step in steps:
                sum_arrival(turn, piece, step).wait_recv()
            count = high - low
            gathered = jnp.concatenate(
                [part[turn, step, low:high].reshape(count * levels, LANES)
                 for step in range(lon_count)], axis=1)
            summed = dot3(gathered, exp).reshape(count, levels, 2 * KMAX)
            result = []
            for slot in range(low, high):
                total_sum = summed[slot - low]
                if turn == 0:
                    total_sum = total_sum + extra[slot]
                result.append(total_sum * keep[order[slot]])
            return result

        def synthesise(parts):
            return dot3(jnp.concatenate(parts, axis=0), syn).reshape(len(parts), levels, width)

        analyse(0, 0)
        rows_arrive(0)
        poles_arrive()
        analyse(0, 1)

        for step in steps:
            col_arrival(0, step).wait_recv()
        col_in[0, 0] = col_out[0]
        place_cols(0)
        packed = [col_in[0, step] for step in range(lon_count)]
        added = [jnp.zeros((levels, 2 * KMAX), F32) for _ in range(rows)]
        for step in range(lon_count):
            behind = packed[step - 1]
            ahead = packed[(step + 1) % lon_count]
            at_last = packed[step] * pltpu.roll(ahead, rows, 1)
            at_first = packed[step] * pltpu.roll(behind, 3 * rows, 1)
            for row in range(rows):
                column = at_last[:, 2 * rows + row:2 * rows + row + 1]
                added[row] = added[row] + column * ends[step, 1:2, :]
                column = at_first[:, 3 * rows + row:3 * rows + row + 1]
                added[row] = added[row] + column * ends[step, 0:1, :]
        for slot in range(rows):
            extra[slot] = added[order[slot]]

        low, high = pieces[0][0]
        filtered = synthesise(collect(0, 0))
        for slot in range(low, high):
            q[order[slot]] = q[order[slot]] + filtered[slot - low]
        analyse(1, 0)

        local = collect(0, 1)
        pole_row = jnp.where(first, local[0], local[1]) * parity
        filtered = synthesise(local + [pole_row])
        q[0] = q[0] + filtered[0]
        q[rows - 1] = q[rows - 1] + filtered[1]

        @pl.when(jnp.logical_not(last))
        def _():
            to_north(1).start()

        @pl.when(jnp.logical_not(first))
        def _():
            to_south(1).start()

        @pl.when(last)
        def _():
            row_second[1, :, :cols] = row_first[1] + filtered[2, :, :cols]

        @pl.when(first)
        def _():
            row_second[0, :, :cols] = row_first[0] + filtered[2, :, :cols]

        rows_arrive(1)
        analyse(1, 1)
        for piece in range(2):
            low, high = pieces[1][piece]
            filtered = synthesise(collect(1, piece))
            for slot in range(low, high):
                row = order[slot]
                out[:, row, :] = q[row, :, :cols] + filtered[slot - low, :, :cols]
        for step in steps:
            col_copy(0, step).wait_send()
            for turn in range(2):
                for piece in range(2):
                    sum_copy(turn, piece, step).wait_send()


def shards(tracer, zonal_courant, north_courant, cutoff):
    levels, rows, cols = tracer.shape
    lat_count = lax.axis_size("lat")
    lon_count = lax.axis_size("lon")
    cap_blocks = lat_count // 8
    width = -(-(cols + 2) // LANES) * LANES
    analysis, expand, synthesis, ends = tables(cols, width, lon_count)
    dma = pltpu.SemaphoreType.DMA
    anywhere = pl.BlockSpec(memory_space=pl.ANY)
    return pl.pallas_call(
        functools.partial(kernel, lat_count, lon_count, cap_blocks),
        out_shape=pltpu.VMEM(tracer.shape, F32),
        in_specs=[pl.BlockSpec(memory_space=pltpu.SMEM)] + [anywhere] * 7,
        out_specs=pl.BlockSpec(memory_space=pltpu.VMEM),
        scratch_shapes=[
            pltpu.VMEM((rows, levels, cols), F32),
            pltpu.VMEM((rows, levels, cols), F32),
            pltpu.VMEM((rows, levels, cols), F32),
            pltpu.VMEM(analysis.shape, BF16),
            pltpu.VMEM(expand.shape, BF16),
            pltpu.VMEM(synthesis.shape, BF16),
            pltpu.VMEM(ends.shape, F32),
            pltpu.VMEM((rows, levels, width), F32),
            pltpu.VMEM((rows, levels, width), F32),
            pltpu.VMEM((2, levels, cols), F32),
            pltpu.VMEM((2, levels, width), F32),
            pltpu.VMEM((2, levels, LANES), F32),
            pltpu.VMEM((2, lon_count, levels, LANES), F32),
            pltpu.VMEM((2, lon_count, rows, levels, LANES), F32),
            pltpu.VMEM((rows, levels, 2 * KMAX), F32),
            dma((3 * rows + 4,)),
            dma((2, 2)), dma((2, 2)), dma((2, lon_count)), dma((2, lon_count)),
            dma((2, 2, lon_count)), dma((2, 2, lon_count)),
        ],
        compiler_params=pltpu.CompilerParams(collective_id=0, has_side_effects=True),
    )(cutoff, tracer, zonal_courant, north_courant,
      jnp.asarray(analysis), jnp.asarray(expand), jnp.asarray(synthesis), jnp.asarray(ends))


def solution(mesh):
    return jax.shard_map(
        shards,
        mesh=mesh,
        in_specs=(P(None, "lat", "lon"), P(None, "lat", "lon"), P(None, "lat", "lon"), P()),
        out_specs=P(None, "lat", "lon"),
        check_vma=False,
    )
```

profile of v0, /device:TPU:0, one launch (start us, length us, event | category | flops | bytes accessed | tf_op | source)
XLA Modules:
  0.0 21.2 jit_solution(14558747822667461524)
XLA Ops:
  0.0 20.5 %shard_map.82 = f32[16,8,720]{2,1,0:T(8,128)S(1)} custom-call(s32[16]{0:T(128)} %cut_ref.1, f32[16,8,720]{2,1,0:T(8,128)} %tracer.1, f32[16,8,720]{2,1,0:T(8,128)} %zonal.1, f32[16,8,720]{2,1,0:T(8,128)} %north.1, bf16[768,256]{1,0:T(8,128)(2,1)} %constant.8.clone.ana_hbm, bf16[2,512,256]{2,1,0:T(8,128)(2,1)} %constant.9.clone.exp_hbm, ...), custom_call_target="tpu_custom_call" | custom-call | tf_op jit(solution)/shard_map/pallas_call | solution.py:457
  20.5 0.7 %copy.10 = f32[16,8,720]{2,1,0:T(8,128)} copy(f32[16,8,720]{2,1,0:T(8,128)S(1)} %shard_map.82) | data formatting | bytes 737280
where the time goes:
time: 21.4 us; the launch traced here: 21.2 us
  Pallas kernels  20.5 us (96%)
  local copies, waits for them, and re-layouts  0.75 us (4%)
    pallas_call x1, Pallas kernels, shards(): pl.pallas_call(functools.partial(kernel, lat_count, lon_count, cap_blocks...  20.5 us
    unnamed x1, local copies, waits for them, and re-layouts  0.75 us

commit v1 on v0

--- a/solution.py
+++ b/solution.py
@@ -82,8 +82,8 @@
 
 def kernel(
     lat_count, lon_count, cap_blocks,
-    cut_ref, tracer, zonal, north, ana_hbm, exp_hbm, syn_hbm, ends_hbm, out,
-    q_in, zc, nc, ana, exp, syn, ends, q, tend,
+    cut_hbm, tracer, zonal, north, ana_hbm, exp_hbm, syn_hbm, ends_hbm, out,
+    cut_ref, q_in, zc, nc, ana, exp, syn, ends, q, tend,
     row_first, row_second, col_out, col_in, part, extra,
     load_sem, row_send, row_recv, col_send, col_recv, sum_send, sum_recv,
 ):
@@ -107,9 +107,9 @@
     for index, (source, target) in enumerate(((tracer, q_in), (zonal, zc), (north, nc))):
         for row in range(rows):
             loads.append(pltpu.make_async_copy(
-                source.at[:, row, :], target.at[row], load_sem.at[index * rows + row]))
-    for load in loads[:rows]:
-        load.start()
+                source.at[:, row, :], target.at[row],
+                load_sem.at[index * rows + row]))
+    cut_in = pltpu.make_async_copy(cut_hbm, cut_ref, load_sem.at[3 * rows + 4])
 
     barrier = pltpu.get_barrier_semaphore()
 
@@ -134,15 +134,20 @@
         greet({"lat": lat, "lon": east})
         greet({"lat": lat, "lon": west})
 
-    for load in loads[rows:]:
-        load.start()
     tables_in = [
         pltpu.make_async_copy(ana_hbm, ana, load_sem.at[3 * rows]),
         pltpu.make_async_copy(exp_hbm, exp, load_sem.at[3 * rows + 1]),
         pltpu.make_async_copy(syn_hbm, syn, load_sem.at[3 * rows + 2]),
         pltpu.make_async_copy(ends_hbm, ends, load_sem.at[3 * rows + 3]),
     ]
-    for load in tables_in:
+    for load in loads[:2 * rows]:
+        load.start()
+
+    @pl.when(polar)
+    def _():
+        tables_in[0].start()
+
+    for load in loads[2 * rows:]:
         load.start()
 
     edge = first.astype(jnp.int32) + last.astype(jnp.int32)
@@ -184,6 +189,11 @@
     @pl.when(jnp.logical_not(first))
     def _():
         to_south(0).start()
+
+    @pl.when(polar)
+    def _():
+        for load in [cut_in] + tables_in[1:]:
+            load.start()
 
     def rows_arrive(turn):
         @pl.when(jnp.logical_not(last))
@@ -307,7 +317,7 @@
         col_out[0] = pack_cols(0)
         for side in (1, lon_count - 1):
             col_copy(0, side).start()
-        for load in loads[rows:] + tables_in:
+        for load in loads[rows:]:
             load.wait()
         for side in (1, lon_count - 1):
             col_arrival(0, side).wait_recv()
@@ -339,15 +349,8 @@
             load.wait()
         col_out[0] = pack_factors(pack_cols(0))
         farthest_first(lambda step: col_copy(0, step).start())
-        for load in loads[2 * rows:] + tables_in:
+        for load in loads[2 * rows:] + tables_in[:1]:
             load.wait()
-
-        offset = jnp.where(
-            lat < cap_blocks, lat * rows, (lat - lat_count + 2 * cap_blocks) * rows)
-        mode = lax.broadcasted_iota(jnp.int32, (1, 2 * KMAX), 1) % KMAX
-        weight = jnp.where(mode == 0, 1.0 / total, 2.0 / total).astype(F32)
-        keep = [jnp.where(mode < cut_ref[offset + row], weight, 0.0) for row in range(rows)]
-        parity = 1.0 - 2.0 * (lax.broadcasted_iota(jnp.int32, (1, 2 * KMAX), 1) % 2).astype(F32)
 
         def analyse(turn, piece):
             low, high = pieces[turn][piece]
@@ -382,6 +385,15 @@
         rows_arrive(0)
         poles_arrive()
         analyse(0, 1)
+
+        for load in tables_in[1:] + [cut_in]:
+            load.wait()
+        offset = jnp.where(
+            lat < cap_blocks, lat * rows, (lat - lat_count + 2 * cap_blocks) * rows)
+        mode = lax.broadcasted_iota(jnp.int32, (1, 2 * KMAX), 1) % KMAX
+        weight = jnp.where(mode == 0, 1.0 / total, 2.0 / total).astype(F32)
+        keep = [jnp.where(mode < cut_ref[offset + row], weight, 0.0) for row in range(rows)]
+        parity = 1.0 - 2.0 * (lax.broadcasted_iota(jnp.int32, (1, 2 * KMAX), 1) % 2).astype(F32)
 
         for step in steps:
             col_arrival(0, step).wait_recv()
@@ -457,9 +469,10 @@
     return pl.pallas_call(
         functools.partial(kernel, lat_count, lon_count, cap_blocks),
         out_shape=pltpu.VMEM(tracer.shape, F32),
-        in_specs=[pl.BlockSpec(memory_space=pltpu.SMEM)] + [anywhere] * 7,
+        in_specs=[anywhere] * 8,
         out_specs=pl.BlockSpec(memory_space=pltpu.VMEM),
         scratch_shapes=[
+            pltpu.SMEM(cutoff.shape, jnp.int32),
             pltpu.VMEM((rows, levels, cols), F32),
             pltpu.VMEM((rows, levels, cols), F32),
             pltpu.VMEM((rows, levels, cols), F32),
@@ -475,7 +488,7 @@
             pltpu.VMEM((2, lon_count, levels, LANES), F32),
             pltpu.VMEM((2, lon_count, rows, levels, LANES), F32),
             pltpu.VMEM((rows, levels, 2 * KMAX), F32),
-            dma((3 * rows + 4,)),
+            dma((3 * rows + 5,)),
             dma((2, 2)), dma((2, 2)), dma((2, lon_count)), dma((2, lon_count)),
             dma((2, 2, lon_count)), dma((2, 2, lon_count)),
         ],

time: 21.4 us -> 21.7 us (1.014)
  Pallas kernels: 20.5 us -> 20.8 us
    pallas_call x1, Pallas kernels: 20.5 us -> 20.8 us  [shards(): pl.pallas_call(functools.partial(kernel, lat_count, lon_count, cap_blocks...]
where the time goes in v1:
time: 21.7 us; the launch traced here: 21.6 us
  Pallas kernels  20.8 us (96%)
  local copies, waits for them, and re-layouts  0.75 us (3%)
    pallas_call x1, Pallas kernels, shards(): pl.pallas_call(functools.partial(kernel, lat_count, lon_count, cap_blocks...  20.8 us
    unnamed x1, local copies, waits for them, and re-layouts  0.75 us

profile of v1, /device:TPU:0, one launch (start us, length us, event | category | flops | bytes accessed | tf_op | source)
XLA Modules:
  0.0 21.6 jit_solution(3568702972432516053)
XLA Ops:
  0.0 20.8 %shard_map.82 = f32[16,8,720]{2,1,0:T(8,128)S(1)} custom-call(s32[16]{0:T(128)} %cut_hbm.1, f32[16,8,720]{2,1,0:T(8,128)} %tracer.1, f32[16,8,720]{2,1,0:T(8,128)} %zonal.1, f32[16,8,720]{2,1,0:T(8,128)} %north.1, bf16[768,256]{1,0:T(8,128)(2,1)} %constant.8.clone.ana_hbm, bf16[2,512,256]{2,1,0:T(8,128)(2,1)} %constant.9.clone.exp_hbm, ...), custom_call_target="tpu_custom_call" | custom-call | tf_op jit(solution)/shard_map/pallas_call | solution.py:469
  20.8 0.7 %copy.10 = f32[16,8,720]{2,1,0:T(8,128)} copy(f32[16,8,720]{2,1,0:T(8,128)S(1)} %shard_map.82) | data formatting | bytes 737280

commit v2 on v1

--- a/solution.py
+++ b/solution.py
@@ -85,7 +85,7 @@
     cut_hbm, tracer, zonal, north, ana_hbm, exp_hbm, syn_hbm, ends_hbm, out,
     cut_ref, q_in, zc, nc, ana, exp, syn, ends, q, tend,
     row_first, row_second, col_out, col_in, part, extra,
-    load_sem, row_send, row_recv, col_send, col_recv, sum_send, sum_recv,
+    load_sem, ready, row_send, row_recv, col_send, col_recv, sum_send, sum_recv,
 ):
     rows, levels, cols = q_in.shape
     width = q.shape[2]
@@ -95,6 +95,11 @@
     polar = jnp.logical_or(lat < cap_blocks, lat >= lat_count - cap_blocks)
     first = lat == 0
     last = lat == lat_count - 1
+    southern = 2 * lat < lat_count
+    border_south = lat == cap_blocks
+    border_north = lat == lat_count - 1 - cap_blocks
+    beyond_south = lat == cap_blocks + 1
+    beyond_north = lat == lat_count - 2 - cap_blocks
     east = lax.rem(lon + 1, lon_count)
     west = lax.rem(lon + lon_count - 1, lon_count)
     across = lax.rem(lon + lon_count // 2, lon_count)
@@ -116,11 +121,11 @@
     def greet(there):
         pl.semaphore_signal(barrier, inc=1, device_id=there, device_id_type=MESH)
 
-    @pl.when(jnp.logical_not(first))
+    @pl.when(jnp.logical_not(jnp.logical_or(first, beyond_south)))
     def _():
         greet({"lat": lat - 1, "lon": lon})
 
-    @pl.when(jnp.logical_not(last))
+    @pl.when(jnp.logical_not(jnp.logical_or(last, beyond_north)))
     def _():
         greet({"lat": lat + 1, "lon": lon})
 
@@ -150,7 +155,8 @@
     for load in loads[2 * rows:]:
         load.start()
 
-    edge = first.astype(jnp.int32) + last.astype(jnp.int32)
+    edge = jnp.logical_or(
+        jnp.logical_or(first, last), jnp.logical_or(border_south, border_north)).astype(jnp.int32)
     sides = jnp.where(polar, lon_count - 1, 2)
     pl.semaphore_wait(barrier, 2 - edge + sides)
 
@@ -182,13 +188,25 @@
     def _():
         over_south().start()
 
-    @pl.when(jnp.logical_not(last))
+    @pl.when(jnp.logical_not(jnp.logical_or(last, border_south)))
     def _():
         to_north(0).start()
 
-    @pl.when(jnp.logical_not(first))
+    @pl.when(jnp.logical_not(jnp.logical_or(first, border_north)))
     def _():
         to_south(0).start()
+
+    def report(there):
+        pl.semaphore_signal(
+            ready, inc=1, device_id={"lat": there, "lon": lon}, device_id_type=MESH)
+
+    @pl.when(beyond_south)
+    def _():
+        report(lat - 1)
+
+    @pl.when(beyond_north)
+    def _():
+        report(lat + 1)
 
     @pl.when(polar)
     def _():
@@ -199,21 +217,37 @@
         @pl.when(jnp.logical_not(last))
         def _():
             to_south(turn).wait_recv()
+
+        @pl.when(jnp.logical_not(first))
+        def _():
+            to_north(turn).wait_recv()
+
+    def rows_left(turn):
+        @pl.when(jnp.logical_not(last))
+        def _():
             to_north(turn).wait_send()
 
         @pl.when(jnp.logical_not(first))
         def _():
-            to_north(turn).wait_recv()
             to_south(turn).wait_send()
+
+    def poles_left():
+        @pl.when(last)
+        def _():
+            over_north().wait_send()
+
+        @pl.when(first)
+        def _():
+            over_south().wait_send()
 
     def poles_arrive():
         @pl.when(last)
         def _():
-            over_north().wait()
+            over_north().wait_recv()
 
         @pl.when(first)
         def _():
-            over_south().wait()
+            over_south().wait_recv()
 
     lane = lax.broadcasted_iota(jnp.int32, (levels, LANES), 1)
     end_tile = (cols - 1) // LANES * LANES
@@ -322,22 +356,57 @@
         for side in (1, lon_count - 1):
             col_arrival(0, side).wait_recv()
         place_cols(0)
-        rows_arrive(0)
-        for row in range(rows):
+        for row in range(1, rows - 1):
             tend[row, :, :cols] = stencil(0, row)
-        for row in range(rows):
+
+        def advance_edge(row):
+            if row:
+                to_south(0).wait_recv()
+            else:
+                to_north(0).wait_recv()
+            q[row, :, :cols] = q[row, :, :cols] + stencil(0, row)
+            if row:
+                to_north(1).start()
+            else:
+                to_south(1).start()
+
+        @pl.when(southern)
+        def _():
+            advance_edge(0)
+
+            @pl.when(border_south)
+            def _():
+                pl.semaphore_wait(ready, 1)
+                to_north(0).start()
+
+            advance_edge(rows - 1)
+
+        @pl.when(jnp.logical_not(southern))
+        def _():
+            advance_edge(rows - 1)
+
+            @pl.when(border_north)
+            def _():
+                pl.semaphore_wait(ready, 1)
+                to_south(0).start()
+
+            advance_edge(0)
+
+        for row in range(1, rows - 1):
             q[row, :, :cols] = q[row, :, :cols] + tend[row, :, :cols]
-        to_north(1).start()
-        to_south(1).start()
         col_out[1] = pack_cols(1)
         for side in (1, lon_count - 1):
             col_copy(1, side).start()
         for side in (1, lon_count - 1):
             col_arrival(1, side).wait_recv()
+        rows_left(1)
+        place_cols(1)
+        for row in range(1, rows - 1):
+            out[:, row, :] = q[row, :, :cols] + stencil(1, row)
         rows_arrive(1)
-        place_cols(1)
-        for row in range(rows):
+        for row in (0, rows - 1):
             out[:, row, :] = q[row, :, :cols] + stencil(1, row)
+        rows_left(0)
         for turn in range(2):
             for side in (1, lon_count - 1):
                 col_copy(turn, side).wait_send()
@@ -450,6 +519,9 @@
             for slot in range(low, high):
                 row = order[slot]
                 out[:, row, :] = q[row, :, :cols] + filtered[slot - low, :, :cols]
+        rows_left(0)
+        rows_left(1)
+        poles_left()
         for step in steps:
             col_copy(0, step).wait_send()
             for turn in range(2):
@@ -488,7 +560,7 @@
             pltpu.VMEM((2, lon_count, levels, LANES), F32),
             pltpu.VMEM((2, lon_count, rows, levels, LANES), F32),
             pltpu.VMEM((rows, levels, 2 * KMAX), F32),
-            dma((3 * rows + 5,)),
+            dma((3 * rows + 5,)), pltpu.SemaphoreType.REGULAR,
             dma((2, 2)), dma((2, 2)), dma((2, lon_count)), dma((2, lon_count)),
             dma((2, 2, lon_count)), dma((2, 2, lon_count)),
         ],

time: 21.7 us -> 19.8 us (0.912)
  Pallas kernels: 20.8 us -> 18.9 us
    pallas_call x1, Pallas kernels: 20.8 us -> 18.9 us  [shards(): pl.pallas_call(functools.partial(kernel, lat_count, lon_count, cap_blocks...]
where the time goes in v2:
time: 19.8 us; the launch traced here: 19.7 us
  Pallas kernels  18.9 us (95%)
  local copies, waits for them, and re-layouts  0.75 us (4%)
    pallas_call x1, Pallas kernels, shards(): pl.pallas_call(functools.partial(kernel, lat_count, lon_count, cap_blocks...  18.9 us
    unnamed x1, local copies, waits for them, and re-layouts  0.75 us

profile of v2, /device:TPU:0, one launch (start us, length us, event | category | flops | bytes accessed | tf_op | source)
XLA Modules:
  0.0 19.7 jit_solution(8963490488661228789)
XLA Ops:
  0.0 18.9 %shard_map.82 = f32[16,8,720]{2,1,0:T(8,128)S(1)} custom-call(s32[16]{0:T(128)} %cut_hbm.1, f32[16,8,720]{2,1,0:T(8,128)} %tracer.1, f32[16,8,720]{2,1,0:T(8,128)} %zonal.1, f32[16,8,720]{2,1,0:T(8,128)} %north.1, bf16[768,256]{1,0:T(8,128)(2,1)} %constant.8.clone.ana_hbm, bf16[2,512,256]{2,1,0:T(8,128)(2,1)} %constant.9.clone.exp_hbm, ...), custom_call_target="tpu_custom_call" | custom-call | tf_op jit(solution)/shard_map/pallas_call | solution.py:541
  18.9 0.7 %copy.10 = f32[16,8,720]{2,1,0:T(8,128)} copy(f32[16,8,720]{2,1,0:T(8,128)S(1)} %shard_map.82) | data formatting | bytes 737280

commit v3 on v2

--- a/solution.py
+++ b/solution.py
@@ -12,6 +12,8 @@
 KMAX = 128
 DIFFUSION = 0.2
 LANES = 128
+QUARTER = LANES // 4
+KEPT = 3 * QUARTER
 MESH = pl.DeviceIdType.MESH
 F32 = jnp.float32
 BF16 = jnp.bfloat16
@@ -43,9 +45,10 @@
 
 def tables(cols, width, lon_count):
     total = cols * lon_count
-    kept = min(LANES, cols)
     basis = np.zeros((width, LANES))
-    basis[:cols, :kept] = window_basis(cols, total)[:, :kept]
+    basis[:cols, :KEPT] = window_basis(cols, total)[:, :KEPT]
+    waves = trig(np.arange(cols), total)
+    assert np.abs(waves - basis[:cols] @ (basis[:cols].T @ waves)).max() < 1e-11
     analysis = np.concatenate(list(split_table(basis)), axis=1)
     expand = np.zeros((lon_count, LANES, 2 * KMAX))
     for step in range(lon_count):
@@ -78,6 +81,33 @@
     size = value.shape[0]
     both = jnp.dot(jnp.concatenate(split(value), axis=0), table[...], preferred_element_type=F32)
     return both[:size, :LANES] + (both[:size, LANES:] + both[size:, :LANES])
+
+
+def packed_tiles(count):
+    return count // 4 * 3 + count % 4
+
+
+def pack(values, lane):
+    tiles = []
+    while len(values) >= 4:
+        fourth = values[3]
+        for place in range(3):
+            moved = pltpu.roll(fourth, KEPT - place * QUARTER, 1)
+            tiles.append(jnp.where(lane >= KEPT, moved, values[place]))
+        values = values[4:]
+    return tiles + values
+
+
+def unpack(tiles, count, lane):
+    values = []
+    while count >= 4:
+        moved = [pltpu.roll(tiles[place], (place + 1) * QUARTER, 1) for place in range(3)]
+        fourth = jnp.where(
+            lane < QUARTER, moved[0], jnp.where(lane < 2 * QUARTER, moved[1], moved[2]))
+        values += tiles[:3] + [fourth]
+        tiles = tiles[3:]
+        count -= 4
+    return values + tiles
 
 
 def kernel(
@@ -107,6 +137,12 @@
     steps = range(1, lon_count)
     order = [0, rows - 1, 1, rows - 2] + list(range(2, rows - 2))
     pieces = (((2, rows), (0, 2)), ((4, rows), (0, 4)))
+    spans = [[], []]
+    for turn in range(2):
+        used = 0
+        for low, high in pieces[turn]:
+            spans[turn].append((used, used + packed_tiles(high - low)))
+            used = spans[turn][-1][1]
 
     loads = []
     for index, (source, target) in enumerate(((tracer, q_in), (zonal, zc), (north, nc))):
@@ -305,14 +341,14 @@
             device_id={"lat": lat, "lon": peers[step]}, device_id_type=MESH)
 
     def sum_copy(turn, piece, step):
-        low, high = pieces[turn][piece]
+        low, high = spans[turn][piece]
         return pltpu.make_async_remote_copy(
             part.at[turn, 0, low:high], part.at[turn, lon_count - step, low:high],
             sum_send.at[turn, piece, step], sum_recv.at[turn, piece, lon_count - step],
             device_id={"lat": lat, "lon": peers[step]}, device_id_type=MESH)
 
     def sum_arrival(turn, piece, step):
-        low, high = pieces[turn][piece]
+        low, high = spans[turn][piece]
         theirs = part.at[turn, step, low:high]
         return pltpu.make_async_remote_copy(
             theirs, theirs, sum_send.at[turn, piece, step], sum_recv.at[turn, piece, step],
@@ -427,7 +463,9 @@
             for slot in range(low, high):
                 tend[slot, :, :cols] = stencil(turn, order[slot])
             found = dot_pair(tend[low:high].reshape(count * levels, width), ana)
-            part[turn, 0, low:high] = found.reshape(count, levels, LANES)
+            tiles = pack([found[row * levels:(row + 1) * levels] for row in range(count)], lane)
+            for place, tile in enumerate(tiles):
+                part[turn, 0, spans[turn][piece][0] + place] = tile
             farthest_first(lambda step: sum_copy(turn, piece, step).start())
 
         def collect(turn, piece):
@@ -435,8 +473,11 @@
             for step in steps:
                 sum_arrival(turn, piece, step).wait_recv()
             count = high - low
+            first_tile, end_tile_at = spans[turn][piece]
             gathered = jnp.concatenate(
-                [part[turn, step, low:high].reshape(count * levels, LANES)
+                [jnp.concatenate(
+                    unpack([part[turn, step, place] for place in range(first_tile, end_tile_at)],
+                           count, lane), axis=0)
                  for step in range(lon_count)], axis=1)
             summed = dot3(gathered, exp).reshape(count, levels, 2 * KMAX)
             result = []

time: 19.8 us -> 19.7 us (level)
  no operation moved by 1% of the time
where the time goes in v3:
time: 19.7 us; the launch traced here: 19.6 us
  Pallas kernels  18.8 us (95%)
  local copies, waits for them, and re-layouts  0.75 us (4%)
    pallas_call x1, Pallas kernels, shards(): pl.pallas_call(functools.partial(kernel, lat_count, lon_count, cap_blocks...  18.8 us
    unnamed x1, local copies, waits for them, and re-layouts  0.75 us

profile of v3, /device:TPU:0, one launch (start us, length us, event | category | flops | bytes accessed | tf_op | source)
XLA Modules:
  0.0 19.6 jit_solution(5940512260640404064)
XLA Ops:
  0.0 18.8 %shard_map.82 = f32[16,8,720]{2,1,0:T(8,128)S(1)} custom-call(s32[16]{0:T(128)} %cut_hbm.1, f32[16,8,720]{2,1,0:T(8,128)} %tracer.1, f32[16,8,720]{2,1,0:T(8,128)} %zonal.1, f32[16,8,720]{2,1,0:T(8,128)} %north.1, bf16[768,256]{1,0:T(8,128)(2,1)} %constant.8.clone.ana_hbm, bf16[2,512,256]{2,1,0:T(8,128)(2,1)} %constant.9.clone.exp_hbm, ...), custom_call_target="tpu_custom_call" | custom-call | tf_op jit(solution)/shard_map/pallas_call | solution.py:582
  18.8 0.7 %copy.10 = f32[16,8,720]{2,1,0:T(8,128)} copy(f32[16,8,720]{2,1,0:T(8,128)S(1)} %shard_map.82) | data formatting | bytes 737280

commit v4 on v3

--- a/solution.py
+++ b/solution.py
@@ -194,7 +194,11 @@
     edge = jnp.logical_or(
         jnp.logical_or(first, last), jnp.logical_or(border_south, border_north)).astype(jnp.int32)
     sides = jnp.where(polar, lon_count - 1, 2)
-    pl.semaphore_wait(barrier, 2 - edge + sides)
+    early = jnp.logical_and(polar, 2 * lon < lon_count)
+    late = jnp.logical_not(early)
+
+    def meet():
+        pl.semaphore_wait(barrier, 2 - edge + sides)
 
     def row_copy(turn, slot, row, there):
         source = tracer.at[:, row, :] if turn == 0 else q.at[row]
@@ -216,21 +220,27 @@
     def over_south():
         return row_copy(0, 0, 0, {"lat": lat, "lon": across})
 
-    @pl.when(last)
-    def _():
-        over_north().start()
-
-    @pl.when(first)
-    def _():
-        over_south().start()
-
-    @pl.when(jnp.logical_not(jnp.logical_or(last, border_south)))
-    def _():
-        to_north(0).start()
-
-    @pl.when(jnp.logical_not(jnp.logical_or(first, border_north)))
-    def _():
-        to_south(0).start()
+    def exchange_rows():
+        @pl.when(last)
+        def _():
+            over_north().start()
+
+        @pl.when(first)
+        def _():
+            over_south().start()
+
+        @pl.when(jnp.logical_not(jnp.logical_or(last, border_south)))
+        def _():
+            to_north(0).start()
+
+        @pl.when(jnp.logical_not(jnp.logical_or(first, border_north)))
+        def _():
+            to_south(0).start()
+
+    @pl.when(late)
+    def _():
+        meet()
+        exchange_rows()
 
     def report(there):
         pl.semaphore_signal(
@@ -453,7 +463,11 @@
         for load in loads[rows:2 * rows]:
             load.wait()
         col_out[0] = pack_factors(pack_cols(0))
-        farthest_first(lambda step: col_copy(0, step).start())
+
+        @pl.when(late)
+        def _():
+            farthest_first(lambda step: col_copy(0, step).start())
+
         for load in loads[2 * rows:] + tables_in[:1]:
             load.wait()
 
@@ -466,6 +480,8 @@
             tiles = pack([found[row * levels:(row + 1) * levels] for row in range(count)], lane)
             for place, tile in enumerate(tiles):
                 part[turn, 0, spans[turn][piece][0] + place] = tile
+
+        def share(turn, piece):
             farthest_first(lambda step: sum_copy(turn, piece, step).start())
 
         def collect(turn, piece):
@@ -492,9 +508,18 @@
             return dot3(jnp.concatenate(parts, axis=0), syn).reshape(len(parts), levels, width)
 
         analyse(0, 0)
+
+        @pl.when(early)
+        def _():
+            meet()
+            exchange_rows()
+            farthest_first(lambda step: col_copy(0, step).start())
+
+        share(0, 0)
         rows_arrive(0)
         poles_arrive()
         analyse(0, 1)
+        share(0, 1)
 
         for load in tables_in[1:] + [cut_in]:
             load.wait()
@@ -529,6 +554,7 @@
         for slot in range(low, high):
             q[order[slot]] = q[order[slot]] + filtered[slot - low]
         analyse(1, 0)
+        share(1, 0)
 
         local = collect(0, 1)
         pole_row = jnp.where(first, local[0], local[1]) * parity
@@ -554,6 +580,7 @@
 
         rows_arrive(1)
         analyse(1, 1)
+        share(1, 1)
         for piece in range(2):
             low, high = pieces[1][piece]
             filtered = synthesise(collect(1, piece))

time: 19.7 us -> 19.7 us (level)
  no operation moved by 1% of the time
where the time goes in v4:
time: 19.7 us; the launch traced here: 19.6 us
  Pallas kernels  18.8 us (95%)
  local copies, waits for them, and re-layouts  0.75 us (4%)
    pallas_call x1, Pallas kernels, shards(): pl.pallas_call(functools.partial(kernel, lat_count, lon_count, cap_blocks...  18.8 us
    unnamed x1, local copies, waits for them, and re-layouts  0.75 us

profile of v4, /device:TPU:0, one launch (start us, length us, event | category | flops | bytes accessed | tf_op | source)
XLA Modules:
  0.0 19.6 jit_solution(11795676353890220745)
XLA Ops:
  0.0 18.8 %shard_map.82 = f32[16,8,720]{2,1,0:T(8,128)S(1)} custom-call(s32[16]{0:T(128)} %cut_hbm.1, f32[16,8,720]{2,1,0:T(8,128)} %tracer.1, f32[16,8,720]{2,1,0:T(8,128)} %zonal.1, f32[16,8,720]{2,1,0:T(8,128)} %north.1, bf16[768,256]{1,0:T(8,128)(2,1)} %constant.8.clone.ana_hbm, bf16[2,512,256]{2,1,0:T(8,128)(2,1)} %constant.9.clone.exp_hbm, ...), custom_call_target="tpu_custom_call" | custom-call | tf_op jit(solution)/shard_map/pallas_call | solution.py:609
  18.8 0.7 %copy.10 = f32[16,8,720]{2,1,0:T(8,128)} copy(f32[16,8,720]{2,1,0:T(8,128)S(1)} %shard_map.82) | data formatting | bytes 737280
